TPU v7x, 32 devices: a whole 2x2x4 slice. The times are simulated.
32 devices in a mesh: groups: 2 (over y), pulse: 4 (over z), range: 2 (over x), sub: 2 (over core).
Axes of the slice: x: 2, y: 2, z: 4, core: 2. Of those that a mesh axis runs over, the one named last changes fastest.
Arguments:
- raw_echo: bfloat16 [2, 128, 16384], P(None, ('groups', 'pulse', 'sub'), 'range'), parts along dimension 1, may hold values from -6 to 6
- range_taps: bfloat16 [32, 512, 128], P('pulse'), may hold values from -0.25 to 0.25
- azim_taps: bfloat16 [128, 2048], P(('groups', 'pulse', 'sub')), parts along dimension 0, may hold values from -1 to 1
- tile_col: int32 [128, 1], P(('groups', 'pulse', 'sub')), parts along dimension 0, may hold values from 0 to 1; in each aligned block of 4 rows (0 to 3, 4 to 7, ...) at most 2 rows name the same one
Outputs:
- image: float32 [2, 8192, 4096], P(None, ('groups', 'pulse', 'range', 'sub')), parts along dimension 1
There are 2 independent parts, one for each index of `groups`. A program takes and returns all parts, laid end to end along the dimension named above; an argument that names none is the same for every part. Nothing has to cross between parts.
Inputs may be any that keep to these rules, and one draw needn't show every extreme that they name: `tile_col`: in each aligned block of 4 pulses no tile column is named by more than 2 pulses.
All inputs are finite; a program needn't handle non-finite values.
Results may differ from a plain program's by a relative error of at most 0.008.
Values may be sent and summed in bfloat16 or wider, within the bound.
No kernel may reach another device: no remote copies, remote signals or barrier semaphores. Data moves between devices by JAX's collectives and lax.ppermute only.
A program may use at most 64 MiB of HBM per device.

v0:
```python
import math
import jax
import jax.numpy as jnp
from jax import lax
from jax.sharding import PartitionSpec as P

CAP = 2


def swapped(block, axis, bit):
    count = lax.axis_size(axis)
    route = []
    for low in range(count):
        high = low | 1 << bit
        if high != low and high < count:
            route += [(low, high), (high, low)]
    return lax.ppermute(block, axis, route)


def as_sent(value):
    return jax.tree.map(lambda a: a.astype(jnp.bfloat16) if a.dtype == jnp.float32 else a, value)


def tables(points, direction):
    indices = jnp.arange(points, dtype=jnp.int32)
    phases = indices[:, None] * indices[None, :] % points
    angles = phases.astype(jnp.float32) * (2.0 * math.pi / points)
    return (jnp.cos(angles), direction * jnp.sin(angles))


def spectral(real_part, imag_part, direction):
    length = real_part.shape[-1]
    outer_len = 1 << (length.bit_length() - 1) // 2
    inner_len = length // outer_len
    leading = real_part.shape[:-1]
    real_part = real_part.reshape(leading + (outer_len, inner_len))
    imag_part = imag_part.reshape(leading + (outer_len, inner_len))
    highest = lax.Precision.HIGHEST
    cos_outer, sin_outer = tables(outer_len, direction)
    mixed_real = jnp.einsum(
        "...nm,nk->...km", real_part, cos_outer, precision=highest
    ) - jnp.einsum("...nm,nk->...km", imag_part, sin_outer, precision=highest)
    mixed_imag = jnp.einsum(
        "...nm,nk->...km", real_part, sin_outer, precision=highest
    ) + jnp.einsum("...nm,nk->...km", imag_part, cos_outer, precision=highest)
    outer_index = jnp.arange(outer_len, dtype=jnp.int32)[:, None]
    inner_index = jnp.arange(inner_len, dtype=jnp.int32)[None, :]
    twists = (outer_index * inner_index % length).astype(jnp.float32) * (2.0 * math.pi / length)
    twist_cos = jnp.cos(twists)
    twist_sin = direction * jnp.sin(twists)
    turned_real = mixed_real * twist_cos - mixed_imag * twist_sin
    turned_imag = mixed_real * twist_sin + mixed_imag * twist_cos
    cos_inner, sin_inner = tables(inner_len, direction)
    final_real = jnp.einsum(
        "...km,mj->...jk", turned_real, cos_inner, precision=highest
    ) - jnp.einsum("...km,mj->...jk", turned_imag, sin_inner, precision=highest)
    final_imag = jnp.einsum(
        "...km,mj->...jk", turned_real, sin_inner, precision=highest
    ) + jnp.einsum("...km,mj->...jk", turned_imag, cos_inner, precision=highest)
    norm_scale = 1.0 / math.sqrt(length)
    return (
        (final_real * norm_scale).reshape(leading + (length,)),
        (final_imag * norm_scale).reshape(leading + (length,)),
    )


def body(raw_echo, range_taps, azim_taps, tile_col):
    n_range = lax.axis_size("range")
    n_pulse = lax.axis_size("pulse")
    my_range = lax.axis_index("range")
    my_sub = lax.axis_index("sub")
    shard_pulses = raw_echo.shape[1]
    shard_samples = raw_echo.shape[2]
    per_device = shard_pulses // n_range
    grouped = raw_echo.reshape(2, n_range, per_device, shard_samples)
    pieces = lax.all_to_all(grouped, "range", split_axis=1, concat_axis=3, tiled=True)
    real_out, imag_out = spectral(
        pieces[0].astype(jnp.float32), pieces[1].astype(jnp.float32), -1.0
    )
    spectrum = jnp.stack([real_out, imag_out]).astype(jnp.bfloat16)
    spectrum = spectrum.reshape(2, per_device, shard_samples * n_range)
    band_bins = spectrum.shape[2] // n_pulse
    first_pulse = my_range * per_device
    cols_here = lax.dynamic_slice_in_dim(tile_col[:, 0], first_pulse, per_device)
    taps_here = lax.dynamic_slice_in_dim(azim_taps, first_pulse, per_device, 0)
    position = jnp.arange(per_device, dtype=jnp.int32)
    earlier = position[None, :] < position[:, None]
    same_tile = cols_here[:, None] == cols_here[None, :]
    slot_rank = jnp.sum(jnp.where(earlier & same_tile, 1, 0), axis=1)
    tile_ids = jnp.arange(n_range, dtype=jnp.int32)
    slot_ids = jnp.arange(CAP, dtype=jnp.int32)
    placing = (
        (cols_here[None, None, :] == tile_ids[:, None, None])
        & (slot_rank[None, None, :] == slot_ids[None, :, None])
    ).astype(jnp.bfloat16)
    banded = spectrum.reshape(2, per_device, n_pulse, band_bins)
    send_lines = jnp.einsum(
        "tcq,xqpb->ptcxb", placing, banded, preferred_element_type=jnp.float32
    ).astype(jnp.bfloat16)
    send_taps = jnp.einsum(
        "tcq,qw->tcw", placing, taps_here, preferred_element_type=jnp.float32
    ).astype(jnp.bfloat16)
    tile_width = send_taps.shape[2]
    send_taps = jnp.broadcast_to(send_taps[None], (n_pulse, n_range, CAP, tile_width))
    block_count, block_bins, block_rows = range_taps.shape
    flat_lines = send_lines.reshape(n_pulse * n_range, CAP, 2, band_bins)
    flat_taps = send_taps.reshape(n_pulse * n_range, CAP, tile_width)
    line_block = lax.all_to_all(
        flat_lines, ("pulse", "range"), split_axis=0, concat_axis=0, tiled=True
    )
    tap_block = lax.all_to_all(
        flat_taps, ("pulse", "range"), split_axis=0, concat_axis=0, tiled=True
    )
    blocked = line_block.reshape(line_block.shape[:3] + (block_count, block_bins))
    resampled = jnp.einsum(
        "skxbr,brj->skxbj", blocked, range_taps, preferred_element_type=jnp.float32
    )
    ky_rows = resampled.reshape(line_block.shape[:3] + (block_count * block_rows,)).astype(
        jnp.bfloat16
    )
    band_rows = ky_rows.shape[3]
    slot_total = ky_rows.shape[0] * ky_rows.shape[1]
    slot_lines = ky_rows.reshape(slot_total, 2, band_rows)
    slot_taps = tap_block.reshape(slot_total, tile_width)
    half_width = tile_width // 2
    other_lines, other_taps = swapped((slot_lines, slot_taps), "sub", 0)
    column_start = my_sub * half_width
    my_taps = lax.dynamic_slice_in_dim(slot_taps, column_start, half_width, 1)
    their_taps = lax.dynamic_slice_in_dim(other_taps, column_start, half_width, 1)
    own_part = jnp.einsum("mi,mxj->xij", my_taps, slot_lines, preferred_element_type=jnp.float32)
    far_part = jnp.einsum(
        "mi,mxj->xij", their_taps, other_lines, preferred_element_type=jnp.float32
    )
    own_round = lax.optimization_barrier(own_part.astype(jnp.bfloat16))
    far_round = lax.optimization_barrier(far_part.astype(jnp.bfloat16))
    kspace = own_round.astype(jnp.float32) + far_round.astype(jnp.float32)
    pieces_each = half_width // n_pulse
    shaped = kspace.reshape(2, n_pulse, pieces_each, band_rows)
    pieces = lax.all_to_all(
        shaped.astype(jnp.bfloat16), "pulse", split_axis=1, concat_axis=3, tiled=True
    ).astype(shaped.dtype)
    real_out, imag_out = spectral(pieces[0], pieces[1], 1.0)
    columns_done = jnp.stack([real_out, imag_out])
    columns_done = columns_done.reshape(2, pieces_each, band_rows * n_pulse)
    moved = lax.all_to_all(
        lax.all_to_all(as_sent(columns_done), "pulse", split_axis=2, concat_axis=1, tiled=True),
        ("range", "sub"),
        split_axis=2,
        concat_axis=1,
        tiled=True,
    ).astype(columns_done.dtype)
    flipped = jnp.swapaxes(moved, 1, 2)
    real_out, imag_out = spectral(flipped[0], flipped[1], 1.0)
    return jnp.stack([real_out, imag_out])


def solution(mesh):
    placed = (
        P(None, ("groups", "pulse", "sub"), "range"),
        P("pulse", None, None),
        P(("groups", "pulse", "sub"), None),
        P(("groups", "pulse", "sub"), None),
    )
    return jax.shard_map(
        body,
        mesh=mesh,
        in_specs=placed,
        out_specs=P(None, ("groups", "pulse", "range", "sub"), None),
        check_vma=False,
    )
```

profile of v0, /device:TPU:0, one launch (start us, length us, event | category | flops | bytes accessed | tf_op | source)
XLA Modules:
  0.0 452.2 jit_solution(6309015719633737124)
XLA Ops:
  0.0 1.3 copy.126
  1.3 0.9 copy.127
  2.2 4.2 all-to-all-start
  7.0 0.7 fusion.182
  8.1 0.9 convolution_convert_fusion.1
  9.0 3.3 all-to-all-done
  13.0 5.1 %all-to-all-start.2 = ((bf16[8,2,2048]{2,1,0:T(2,128)(2,1)}), bf16[8,2,2048]{2,1,0:T(2,128)(2,1)S(1)}, u32[]{:S(2)}, u32[]{:S(2)}) async-start(bf16[8,2,2048]{2,1,0:T(2,128)(2,1)} %bitcast.30), calls=%async_computation.2 | async-start | bytes 131072 | tf_op jit(solution)/shard_map/all_to_all | solution.py:111
  24.2 1.0 copy.134
  25.2 6.3 %all-to-all-start.1 = ((bf16[8,2,2,4096]{3,2,1,0:T(2,128)(2,1)}), bf16[8,2,2,4096]{3,2,1,0:T(2,128)(2,1)S(1)}, u32[]{:S(2)}, u32[]{:S(2)}) async-start(bf16[8,2,2,4096]{3,2,1,0:T(2,128)(2,1)} %copy.134), calls=%async_computation.1 | async-start | bytes 524288 | tf_op jit(solution)/shard_map/all_to_all | solution.py:108
  31.6 8.1 %all-to-all-done.1 = bf16[8,2,2,4096]{3,2,1,0:T(2,128)(2,1)S(1)} async-done(((bf16[8,2,2,4096]{3,2,1,0:T(2,128)(2,1)}), bf16[8,2,2,4096]{3,2,1,0:T(2,128)(2,1)S(1)}, u32[]{:S(2)}, u32[]{:S(2)}) %all-to-all-start.1) | async-done | bytes 262176 | tf_op jit(solution)/shard_map/all_to_all | solution.py:108
  40.4 1.3 convert_bitcast_fusion.1
  41.7 1.3 convert_bitcast_fusion
  42.9 2.2 add_convert_fusion
  45.2 2.3 copy.221
  47.5 5.4 %all-to-all-start.3 = ((bf16[2,4,256,1024]{2,3,0,1:T(8,128)(2,1)}), bf16[2,4,256,1024]{2,3,0,1:T(8,128)(2,1)}, u32[]{:S(2)}, u32[]{:S(2)}) async-start(bf16[2,4,256,1024]{2,3,0,1:T(8,128)(2,1)} %bitcast.216), calls=%async_computation.3 | async-start | bytes 8388608 | tf_op jit(solution)/shard_map/all_to_all | solution.py:139
  53.0 93.5 %all-to-all-done.3 = bf16[2,4,256,1024]{2,3,0,1:T(8,128)(2,1)} async-done(((bf16[2,4,256,1024]{2,3,0,1:T(8,128)(2,1)}), bf16[2,4,256,1024]{2,3,0,1:T(8,128)(2,1)}, u32[]{:S(2)}, u32[]{:S(2)}) %all-to-all-start.3) | async-done | bytes 4194336 | tf_op jit(solution)/shard_map/all_to_all | solution.py:139
  146.5 2.5 copy.222
  149.2 2.8 fusion.38
  152.0 2.8 fusion.40
  154.9 2.9 convolution_add_fusion.1
  157.7 4.7 %fusion.1 = (f32[256,64,64]{0,1,2:T(8,128)S(1)}, f32[256,64,64]{0,1,2:T(8,128)S(1)}) fusion(f32[64,256,64]{1,0,2:T(8,128)S(1)} %convolution_add_fusion.1, f32[64,64]{0,1:T(8,128)S(1)} %get-tuple-element.17, f32[64,64]{0,1:T(8,128)S(1)} %get-tuple-element.18, f32[64,256,64]{1,0,2:T(8,128)S(1)} %fusion.40, bf16[256,64,64]{0,2,1:T(8,128)(2,1)S(1)} %bitcast.210), kind=kOutput, calls=%fused_computation.8 | convolution fusion | flops 812703744 | bytes 18907136 | tf_op jit(solution)/shard_map/...nm,nk->...km/dot_general | solution.py:42
  162.4 6.3 %fusion.12 = f32[64,256,64]{1,0,2:T(8,128)S(1)} fusion(f32[256,64,64]{0,1,2:T(8,128)S(1)} %get-tuple-element.8), kind=kOutput, calls=%fused_computation.30 | convolution fusion | flops 805363712 | bytes 8388608 | tf_op jit(solution)/shard_map/...km,mj->...jk/dot_general | solution.py:59
  168.7 6.5 %fusion.14 = f32[64,256,64]{1,0,2:T(8,128)S(1)} fusion(f32[256,64,64]{0,1,2:T(8,128)S(1)} %get-tuple-element.8), kind=kOutput, calls=%fused_computation.32 | convolution fusion | flops 805363712 | bytes 8388608 | tf_op jit(solution)/shard_map/...km,mj->...jk/dot_general | solution.py:56
  175.2 6.0 %fusion.25 = bf16[1,256,64,64]{1,2,3,0:T(8,128)(2,1)S(1)} fusion(f32[64,256,64]{1,0,2:T(8,128)S(1)} %fusion.12, f32[256,64,64]{0,1,2:T(8,128)S(1)} %get-tuple-element.7), kind=kOutput, calls=%fused_computation.44 | convolution fusion | flops 808509440 | bytes 10485760 | tf_op jit(solution)/shard_map/...km,mj->...jk/dot_general | solution.py:57
  181.2 1.2 copy.149
  182.4 5.9 %fusion.24 = bf16[1,256,64,64]{1,2,3,0:T(8,128)(2,1)S(1)} fusion(f32[64,256,64]{1,0,2:T(8,128)S(1)} %fusion.14, f32[256,64,64]{0,1,2:T(8,128)S(1)} %get-tuple-element.7), kind=kOutput, calls=%fused_computation.43 | convolution fusion | flops 808509440 | bytes 10485760 | tf_op jit(solution)/shard_map/...km,mj->...jk/dot_general | solution.py:54
  188.3 1.2 copy.146
  189.9 25.5 %copy.150 = bf16[2,256,4096]{1,0,2:T(2,128)(2,1)S(1)} copy(bf16[2,256,4096]{1,2,0:T(8,128)(2,1)S(1)} %maximum_bitcast_fusion) | data formatting | bytes 8388608 | tf_op jit(solution)/shard_map/convert_element_type | solution.py:21
  215.4 95.8 %all_to_all.76 = bf16[2,256,4096]{1,0,2:T(2,128)(2,1)S(1)} all-to-all(bf16[2,256,4096]{1,0,2:T(2,128)(2,1)S(1)} %copy.150), channel_id=1, replica_groups=mesh['groups'=2,'pulse'=4,'range'=2,'sub'=2] {'pulse'}, dimensions={2} | all-to-all | bytes 8388608 | tf_op jit(solution)/shard_map/all_to_all | solution.py:146
  311.2 2.6 copy.151
  313.7 6.3 %copy.152 = bf16[2,4,256,1024]{3,2,1,0:T(8,128)(2,1)} copy(bf16[2,4,256,1024]{2,3,1,0:T(8,128)(2,1)} %bitcast.219) | data formatting | bytes 8388608 | tf_op jit(solution)/shard_map/all_to_all | solution.py:146
  320.0 11.3 %copy.153 = bf16[2,1024,1024]{1,0,2:T(2,128)(2,1)} copy(bf16[2,1024,1024]{2,1,0:T(8,128)(2,1)} %bitcast.220) | data formatting | bytes 8388608 | tf_op jit(solution)/shard_map/all_to_all | solution.py:146
  331.2 51.9 %all_to_all.77 = bf16[2,1024,1024]{1,0,2:T(2,128)(2,1)S(1)} all-to-all(bf16[2,1024,1024]{1,0,2:T(2,128)(2,1)} %copy.153), channel_id=1, replica_groups=mesh['groups'=2,'pulse'=4,'range'=2,'sub'=2] {'range','sub'}, dimensions={2} | all-to-all | bytes 8388608 | tf_op jit(solution)/shard_map/all_to_all | solution.py:145
  383.1 3.3 copy.154
  386.5 6.4 %copy.155 = bf16[2,4,1024,256]{3,2,1,0:T(8,128)(2,1)} copy(bf16[2,4,1024,256]{2,3,1,0:T(8,128)(2,1)} %bitcast.221) | data formatting | bytes 8388608 | tf_op jit(solution)/shard_map/all_to_all | solution.py:145
  392.8 2.5 fusion.260
  395.3 2.8 fusion.32
  398.1 2.8 fusion.34
  401.0 2.9 convolution_add_fusion
  403.9 4.7 %subtract_bitcast_fusion = (f32[256,64,64]{0,1,2:T(8,128)S(1)}, f32[256,64,64]{0,1,2:T(8,128)S(1)}) fusion(f32[64,256,64]{1,0,2:T(8,128)S(1)} %convolution_add_fusion, f32[64,64]{0,1:T(8,128)S(1)} %get-tuple-element.17, f32[64,64]{0,1:T(8,128)S(1)} %get-tuple-element.18, f32[64,256,64]{1,0,2:T(8,128)S(1)} %fusion.34, bf16[256,64,64]{0,2,1:T(8,128)(2,1)S(1)} %bitcast.208), kind=kOutput, calls=%fused_computation.17 | convolution fusion | flops 812703744 | bytes 18907136 | tf_op jit(solution)/shard_map/...nm,nk->...km/dot_general | solution.py:42
  408.6 6.0 %fusion.4 = f32[64,256,64]{1,0,2:T(8,128)S(1)} fusion(f32[256,64,64]{0,1,2:T(8,128)S(1)} %get-tuple-element.6), kind=kOutput, calls=%fused_computation.22 | convolution fusion | flops 805363712 | bytes 8388608 | tf_op jit(solution)/shard_map/...km,mj->...jk/dot_general | solution.py:59
  414.6 6.7 %fusion.6 = f32[64,256,64]{1,0,2:T(8,128)S(1)} fusion(f32[256,64,64]{0,1,2:T(8,128)S(1)} %get-tuple-element.6), kind=kOutput, calls=%fused_computation.24 | convolution fusion | flops 805363712 | bytes 8388608 | tf_op jit(solution)/shard_map/...km,mj->...jk/dot_general | solution.py:56
  421.3 6.4 %multiply_bitcast_fusion.1 = f32[256,64,64]{0,1,2:T(8,128)S(1)} fusion(f32[64,256,64]{1,0,2:T(8,128)S(1)} %fusion.6, f32[256,64,64]{0,1,2:T(8,128)S(1)} %get-tuple-element.5), kind=kOutput, calls=%fused_computation.15 | convolution fusion | flops 807460864 | bytes 12582912 | tf_op jit(solution)/shard_map/...km,mj->...jk/dot_general | solution.py:54
  427.7 6.7 %multiply_bitcast_fusion = f32[256,64,64]{0,1,2:T(8,128)S(1)} fusion(f32[64,256,64]{1,0,2:T(8,128)S(1)} %fusion.4, f32[256,64,64]{0,1,2:T(8,128)S(1)} %get-tuple-element.5), kind=kOutput, calls=%fused_computation.14 | convolution fusion | flops 807460864 | bytes 12582912 | tf_op jit(solution)/shard_map/...km,mj->...jk/dot_general | solution.py:57
  434.4 2.4 copy.165
  436.9 2.4 copy.162
  439.3 3.8 pad_maximum_fusion
  443.1 9.0 %copy.166 = f32[2,256,4096]{2,1,0:T(8,128)} copy(f32[2,256,4096]{1,2,0:T(8,128)} %pad_maximum_fusion) | data formatting | bytes 16777216 | tf_op jit(solution)/shard_map/stack | solution.py:154
  (42 shorter events, 9.1 us)
Async XLA Ops:
  0.0 39.9 %copy-start = (bf16[8,512,128]{2,1,0:T(8,128)(2,1)S(1)}, bf16[8,512,128]{2,1,0:T(8,128)(2,1)}, u32[]{:S(2)}) copy-start(bf16[8,512,128]{2,1,0:T(8,128)(2,1)} %param.5) | copy-start | bytes 3145732
  2.2 10.1 %all-to-all-start = ((bf16[2,2,4,8192]{3,2,0,1:T(4,128)(2,1)}), bf16[2,2,4,8192]{3,2,0,1:T(4,128)(2,1)S(1)}, u32[]{:S(2)}, u32[]{:S(2)}) async-start(bf16[2,2,4,8192]{3,2,0,1:T(4,128)(2,1)} %copy.127), calls=%async_computation | async-start | bytes 524288 | tf_op jit(solution)/shard_map/all_to_all | solution.py:76
  13.0 12.2 %all-to-all-start.2 = ((bf16[8,2,2048]{2,1,0:T(2,128)(2,1)}), bf16[8,2,2048]{2,1,0:T(2,128)(2,1)S(1)}, u32[]{:S(2)}, u32[]{:S(2)}) async-start(bf16[8,2,2048]{2,1,0:T(2,128)(2,1)} %bitcast.30), calls=%async_computation.2 | async-start | bytes 131072 | tf_op jit(solution)/shard_map/all_to_all | solution.py:111
  25.2 14.5 %all-to-all-start.1 = ((bf16[8,2,2,4096]{3,2,1,0:T(2,128)(2,1)}), bf16[8,2,2,4096]{3,2,1,0:T(2,128)(2,1)S(1)}, u32[]{:S(2)}, u32[]{:S(2)}) async-start(bf16[8,2,2,4096]{3,2,1,0:T(2,128)(2,1)} %copy.134), calls=%async_computation.1 | async-start | bytes 524288 | tf_op jit(solution)/shard_map/all_to_all | solution.py:108
  31.5 10.1 %collective-permute-start.1 = (bf16[16,2048]{1,0:T(8,128)(2,1)S(1)}, bf16[16,2048]{1,0:T(8,128)(2,1)S(1)}, u32[]{:S(2)}, u32[]{:S(2)}) collective-permute-start(bf16[16,2048]{1,0:T(8,128)(2,1)S(1)} %reshape.306), channel_id=1, source_target_pairs={{0,1},{1,0},{2,3},{3,2},{4,5},{5,4},{6,7},{7,6},{8,9},{9,8},{10,11... | collective-permute-start | bytes 196616 | tf_op jit(solution)/shard_map/ppermute | solution.py:17
  40.3 1.4 collective-permute-start
  47.5 99.0 %all-to-all-start.3 = ((bf16[2,4,256,1024]{2,3,0,1:T(8,128)(2,1)}), bf16[2,4,256,1024]{2,3,0,1:T(8,128)(2,1)}, u32[]{:S(2)}, u32[]{:S(2)}) async-start(bf16[2,4,256,1024]{2,3,0,1:T(8,128)(2,1)} %bitcast.216), calls=%async_computation.3 | async-start | bytes 8388608 | tf_op jit(solution)/shard_map/all_to_all | solution.py:139
  443.1 9.0 %copy-start.1 = (bf16[8,512,128]{2,1,0:T(8,128)(2,1)S(1)}, bf16[8,512,128]{2,1,0:T(8,128)(2,1)}, u32[]{:S(2)}) copy-start(bf16[8,512,128]{2,1,0:T(8,128)(2,1)} %param.5) | copy-start | bytes 3145732
where the time goes:
time: 459 us; the launch traced here: 452 us
  blocking collectives  148 us (32%)
  waiting for transfers between devices  105 us (23%)
  matrix products  85.8 us (19%)
  local copies, waits for them, and re-layouts  84.9 us (18%)
  starting transfers between devices  21.2 us (5%)
  other arithmetic  7.26 us (2%)
    all_to_all x1, blocking collectives, body(): lax.all_to_all(as_sent(columns_done), 'pulse', split_axis=2, concat_axis=...  95.8 us
    all_to_all x1, waiting for transfers between devices, body(): lax.all_to_all(shaped.astype(jnp.bfloat16), 'pulse', split_axis=1, concat...  93.5 us
    all_to_all x1, blocking collectives, body(): lax.all_to_all(lax.all_to_all(as_sent(columns_done), 'pulse', split_axis=...  51.9 us
    convert_element_type x1, local copies, waits for them, and re-layouts, as_sent(): a.astype(jnp.bfloat16)  25.5 us
    all_to_all x3, local copies, waits for them, and re-layouts, body(): lax.all_to_all(as_sent(columns_done), 'pulse', split_axis=2, concat_axis=...  20.1 us
    dot_general x3, matrix products, spectral(): jnp.einsum('...km,mj->...jk', turned_imag, sin_inner, precision=highest)  13.9 us
    dot_general x3, matrix products, spectral(): jnp.einsum('...km,mj->...jk', turned_real, sin_inner, precision=highest)  13.4 us
    dot_general x3, matrix products, spectral(): jnp.einsum('...km,mj->...jk', turned_imag, cos_inner, precision=highest)  13 us
  transfers between devices with their start and end apart: 6, of which 3 were waited for; matrix products, arithmetic and copies ran while one was open for 3% of the time, Pallas kernels for 0%

commit v1 on v0

--- a/solution.py
+++ b/solution.py
@@ -5,6 +5,13 @@
 from jax.sharding import PartitionSpec as P
 
 CAP = 2
+
+
+def trade_parts(x, name, split, join):
+    size = lax.axis_size(name)
+    blocks = jnp.stack(jnp.split(x, size, axis=split), axis=0)
+    blocks = lax.all_to_all(blocks, name, split_axis=0, concat_axis=0)
+    return jnp.concatenate(blocks, axis=join)
 
 
 def swapped(block, axis, bit):
@@ -142,12 +149,11 @@
     real_out, imag_out = spectral(pieces[0], pieces[1], 1.0)
     columns_done = jnp.stack([real_out, imag_out])
     columns_done = columns_done.reshape(2, pieces_each, band_rows * n_pulse)
-    moved = lax.all_to_all(
+    moved = trade_parts(
         lax.all_to_all(as_sent(columns_done), "pulse", split_axis=2, concat_axis=1, tiled=True),
         ("range", "sub"),
-        split_axis=2,
-        concat_axis=1,
-        tiled=True,
+        2,
+        1,
     ).astype(columns_done.dtype)
     flipped = jnp.swapaxes(moved, 1, 2)
     real_out, imag_out = spectral(flipped[0], flipped[1], 1.0)

time: 459 us -> 437 us (0.952)
  local copies, waits for them, and re-layouts: 84.9 us -> 64.5 us
    all_to_all x3 -> x2, local copies, waits for them, and re-layouts: 20.1 us -> 8.85 us  [body(): lax.all_to_all(as_sent(columns_done), 'pulse', split_axis=2, concat_axis=...]
    all_to_all x2 -> x0, local copies, waits for them, and re-layouts: 9.69 us -> none  [body(): lax.all_to_all(lax.all_to_all(as_sent(columns_done), 'pulse', split_axis=...]
where the time goes in v1:
time: 437 us; the launch traced here: 431 us
  blocking collectives  146 us (33%)
  waiting for transfers between devices  105 us (24%)
  matrix products  85.4 us (20%)
  local copies, waits for them, and re-layouts  64.5 us (15%)
  starting transfers between devices  21 us (5%)
  other arithmetic  7.83 us (2%)
    all_to_all x1, blocking collectives, body(): lax.all_to_all(as_sent(columns_done), 'pulse', split_axis=2, concat_axis=...  95.8 us
    all_to_all x1, waiting for transfers between devices, body(): lax.all_to_all(shaped.astype(jnp.bfloat16), 'pulse', split_axis=1, concat...  93.6 us
    all_to_all x1, blocking collectives, trade_parts(): blocks = lax.all_to_all(blocks, name, split_axis=0, concat_axis=0)  50.7 us
    convert_element_type x1, local copies, waits for them, and re-layouts, as_sent(): a.astype(jnp.bfloat16)  25.5 us
    dot_general x3, matrix products, spectral(): jnp.einsum('...km,mj->...jk', turned_real, sin_inner, precision=highest)  13.5 us
    dot_general x3, matrix products, spectral(): jnp.einsum('...km,mj->...jk', turned_imag, sin_inner, precision=highest)  13.5 us
    dot_general x3, matrix products, spectral(): jnp.einsum('...km,mj->...jk', turned_imag, cos_inner, precision=highest)  13 us
    dot_general x3, matrix products, spectral(): jnp.einsum('...km,mj->...jk', turned_real, cos_inner, precision=highest)  12.9 us
  transfers between devices with their start and end apart: 6, of which 3 were waited for; matrix products, arithmetic and copies ran while one was open for 3% of the time, Pallas kernels for 0%

profile of v1, /device:TPU:0, one launch (start us, length us, event | category | flops | bytes accessed | tf_op | source)
XLA Modules:
  0.0 431.1 jit_solution(9116974509237830483)
XLA Ops:
  0.0 1.3 copy.124
  1.3 0.9 copy.125
  2.2 4.2 all-to-all-start
  7.0 0.7 fusion.182
  8.1 0.9 convolution_convert_fusion.1
  9.0 3.3 all-to-all-done
  13.0 5.1 %all-to-all-start.2 = ((bf16[8,2,2048]{2,1,0:T(2,128)(2,1)}), bf16[8,2,2048]{2,1,0:T(2,128)(2,1)S(1)}, u32[]{:S(2)}, u32[]{:S(2)}) async-start(bf16[8,2,2048]{2,1,0:T(2,128)(2,1)} %bitcast.30), calls=%async_computation.2 | async-start | bytes 131072 | tf_op jit(solution)/shard_map/all_to_all | solution.py:118
  20.7 0.7 fusion.57
  22.1 0.7 fusion.48
  22.9 0.7 fusion.49
  24.2 1.0 copy.132
  25.2 6.2 %all-to-all-start.1 = ((bf16[8,2,2,4096]{3,2,1,0:T(2,128)(2,1)}), bf16[8,2,2,4096]{3,2,1,0:T(2,128)(2,1)S(1)}, u32[]{:S(2)}, u32[]{:S(2)}) async-start(bf16[8,2,2,4096]{3,2,1,0:T(2,128)(2,1)} %copy.132), calls=%async_computation.1 | async-start | bytes 524288 | tf_op jit(solution)/shard_map/all_to_all | solution.py:115
  31.6 8.1 %all-to-all-done.1 = bf16[8,2,2,4096]{3,2,1,0:T(2,128)(2,1)S(1)} async-done(((bf16[8,2,2,4096]{3,2,1,0:T(2,128)(2,1)}), bf16[8,2,2,4096]{3,2,1,0:T(2,128)(2,1)S(1)}, u32[]{:S(2)}, u32[]{:S(2)}) %all-to-all-start.1) | async-done | bytes 262176 | tf_op jit(solution)/shard_map/all_to_all | solution.py:115
  40.3 1.3 convert_bitcast_fusion.1
  41.6 1.3 convert_bitcast_fusion
  42.9 2.2 add_convert_fusion
  45.1 2.3 copy.217
  47.4 5.3 %all-to-all-start.3 = ((bf16[2,4,256,1024]{2,3,0,1:T(8,128)(2,1)}), bf16[2,4,256,1024]{2,3,0,1:T(8,128)(2,1)}, u32[]{:S(2)}, u32[]{:S(2)}) async-start(bf16[2,4,256,1024]{2,3,0,1:T(8,128)(2,1)} %bitcast.222), calls=%async_computation.3 | async-start | bytes 8388608 | tf_op jit(solution)/shard_map/all_to_all | solution.py:146
  52.8 93.6 %all-to-all-done.3 = bf16[2,4,256,1024]{2,3,0,1:T(8,128)(2,1)} async-done(((bf16[2,4,256,1024]{2,3,0,1:T(8,128)(2,1)}), bf16[2,4,256,1024]{2,3,0,1:T(8,128)(2,1)}, u32[]{:S(2)}, u32[]{:S(2)}) %all-to-all-start.3) | async-done | bytes 4194336 | tf_op jit(solution)/shard_map/all_to_all | solution.py:146
  146.4 2.5 copy.218
  149.2 2.8 fusion.38
  152.0 2.8 fusion.40
  154.8 2.9 convolution_add_fusion.1
  157.7 4.7 %fusion.1 = (f32[256,64,64]{0,1,2:T(8,128)S(1)}, f32[256,64,64]{0,1,2:T(8,128)S(1)}) fusion(f32[64,256,64]{1,0,2:T(8,128)S(1)} %convolution_add_fusion.1, f32[64,64]{0,1:T(8,128)S(1)} %get-tuple-element.21, f32[64,64]{0,1:T(8,128)S(1)} %get-tuple-element.22, f32[64,256,64]{1,0,2:T(8,128)S(1)} %fusion.40, bf16[256,64,64]{0,2,1:T(8,128)(2,1)S(1)} %bitcast.216), kind=kOutput, calls=%fused_computation.9 | convolution fusion | flops 812703744 | bytes 18907136 | tf_op jit(solution)/shard_map/...nm,nk->...km/dot_general | solution.py:49
  162.4 6.3 %fusion.12 = f32[64,256,64]{1,0,2:T(8,128)S(1)} fusion(f32[256,64,64]{0,1,2:T(8,128)S(1)} %get-tuple-element.8), kind=kOutput, calls=%fused_computation.31 | convolution fusion | flops 805363712 | bytes 8388608 | tf_op jit(solution)/shard_map/...km,mj->...jk/dot_general | solution.py:66
  168.7 6.3 %fusion.14 = f32[64,256,64]{1,0,2:T(8,128)S(1)} fusion(f32[256,64,64]{0,1,2:T(8,128)S(1)} %get-tuple-element.8), kind=kOutput, calls=%fused_computation.33 | convolution fusion | flops 805363712 | bytes 8388608 | tf_op jit(solution)/shard_map/...km,mj->...jk/dot_general | solution.py:63
  175.0 6.0 %fusion.25 = bf16[1,256,64,64]{1,2,3,0:T(8,128)(2,1)S(1)} fusion(f32[64,256,64]{1,0,2:T(8,128)S(1)} %fusion.12, f32[256,64,64]{0,1,2:T(8,128)S(1)} %get-tuple-element.7), kind=kOutput, calls=%fused_computation.45 | convolution fusion | flops 808509440 | bytes 10485760 | tf_op jit(solution)/shard_map/...km,mj->...jk/dot_general | solution.py:64
  181.0 1.2 copy.147
  182.2 5.9 %fusion.24 = bf16[1,256,64,64]{1,2,3,0:T(8,128)(2,1)S(1)} fusion(f32[64,256,64]{1,0,2:T(8,128)S(1)} %fusion.14, f32[256,64,64]{0,1,2:T(8,128)S(1)} %get-tuple-element.7), kind=kOutput, calls=%fused_computation.44 | convolution fusion | flops 808509440 | bytes 10485760 | tf_op jit(solution)/shard_map/...km,mj->...jk/dot_general | solution.py:61
  188.1 1.2 copy.144
  189.7 25.5 %copy.148 = bf16[2,256,4096]{1,0,2:T(2,128)(2,1)S(1)} copy(bf16[2,256,4096]{1,2,0:T(8,128)(2,1)S(1)} %maximum_bitcast_fusion) | data formatting | bytes 8388608 | tf_op jit(solution)/shard_map/convert_element_type | solution.py:28
  215.1 95.8 %all_to_all.63 = bf16[2,256,4096]{1,0,2:T(2,128)(2,1)S(1)} all-to-all(bf16[2,256,4096]{1,0,2:T(2,128)(2,1)S(1)} %copy.148), channel_id=1, replica_groups=mesh['groups'=2,'pulse'=4,'range'=2,'sub'=2] {'pulse'}, dimensions={2} | all-to-all | bytes 8388608 | tf_op jit(solution)/shard_map/all_to_all | solution.py:153
  310.9 2.6 copy.149
  313.5 6.3 %copy.150 = bf16[2,4,256,1024]{3,2,1,0:T(8,128)(2,1)} copy(bf16[2,4,256,1024]{2,3,1,0:T(8,128)(2,1)} %bitcast.226) | data formatting | bytes 8388608 | tf_op jit(solution)/shard_map/all_to_all | solution.py:153
  319.7 2.5 slice_bitcast_fusion.3
  322.8 50.7 %all_to_all.64 = bf16[4,2,1024,256]{3,2,1,0:T(8,128)(2,1)S(1)} all-to-all(bf16[4,2,1024,256]{3,2,1,0:T(8,128)(2,1)S(1)} %pad_maximum_fusion.1), channel_id=1, replica_groups=mesh['groups'=2,'pulse'=4,'range'=2,'sub'=2] {'range','sub'}, dimensions={0} | all-to-all | bytes 8388608 | tf_op jit(solution)/shard_map/all_to_all | solution.py:13
  374.1 2.8 fusion.32
  376.9 2.8 fusion.34
  379.7 2.9 convolution_add_fusion
  382.6 4.7 %subtract_bitcast_fusion = (f32[256,64,64]{0,1,2:T(8,128)S(1)}, f32[256,64,64]{0,1,2:T(8,128)S(1)}) fusion(f32[64,256,64]{1,0,2:T(8,128)S(1)} %convolution_add_fusion, f32[64,64]{0,1:T(8,128)S(1)} %get-tuple-element.21, f32[64,64]{0,1:T(8,128)S(1)} %get-tuple-element.22, f32[64,256,64]{1,0,2:T(8,128)S(1)} %fusion.34, bf16[256,64,64]{0,2,1:T(8,128)(2,1)S(1)} %bitcast.214), kind=kOutput, calls=%fused_computation.18 | convolution fusion | flops 812703744 | bytes 18907136 | tf_op jit(solution)/shard_map/...nm,nk->...km/dot_general | solution.py:49
  387.3 6.0 %fusion.4 = f32[64,256,64]{1,0,2:T(8,128)S(1)} fusion(f32[256,64,64]{0,1,2:T(8,128)S(1)} %get-tuple-element.6), kind=kOutput, calls=%fused_computation.23 | convolution fusion | flops 805363712 | bytes 8388608 | tf_op jit(solution)/shard_map/...km,mj->...jk/dot_general | solution.py:66
  393.3 6.5 %fusion.6 = f32[64,256,64]{1,0,2:T(8,128)S(1)} fusion(f32[256,64,64]{0,1,2:T(8,128)S(1)} %get-tuple-element.6), kind=kOutput, calls=%fused_computation.25 | convolution fusion | flops 805363712 | bytes 8388608 | tf_op jit(solution)/shard_map/...km,mj->...jk/dot_general | solution.py:63
  399.8 6.4 %multiply_bitcast_fusion.1 = f32[256,64,64]{0,1,2:T(8,128)S(1)} fusion(f32[64,256,64]{1,0,2:T(8,128)S(1)} %fusion.6, f32[256,64,64]{0,1,2:T(8,128)S(1)} %get-tuple-element.5), kind=kOutput, calls=%fused_computation.16 | convolution fusion | flops 807460864 | bytes 12582912 | tf_op jit(solution)/shard_map/...km,mj->...jk/dot_general | solution.py:61
  406.2 6.8 %multiply_bitcast_fusion = f32[256,64,64]{0,1,2:T(8,128)S(1)} fusion(f32[64,256,64]{1,0,2:T(8,128)S(1)} %fusion.4, f32[256,64,64]{0,1,2:T(8,128)S(1)} %get-tuple-element.5), kind=kOutput, calls=%fused_computation.15 | convolution fusion | flops 807460864 | bytes 12582912 | tf_op jit(solution)/shard_map/...km,mj->...jk/dot_general | solution.py:64
  413.0 2.4 copy.161
  415.5 2.4 copy.158
  417.9 3.8 pad_maximum_fusion
  421.7 9.0 %copy.162 = f32[2,256,4096]{2,1,0:T(8,128)} copy(f32[2,256,4096]{1,2,0:T(8,128)} %pad_maximum_fusion) | data formatting | bytes 16777216 | tf_op jit(solution)/shard_map/stack | solution.py:160
  (42 shorter events, 8.2 us)
Async XLA Ops:
  0.0 39.8 %copy-start = (bf16[8,512,128]{2,1,0:T(8,128)(2,1)S(1)}, bf16[8,512,128]{2,1,0:T(8,128)(2,1)}, u32[]{:S(2)}) copy-start(bf16[8,512,128]{2,1,0:T(8,128)(2,1)} %param.5) | copy-start | bytes 3145732
  2.2 10.1 %all-to-all-start = ((bf16[2,2,4,8192]{3,2,0,1:T(4,128)(2,1)}), bf16[2,2,4,8192]{3,2,0,1:T(4,128)(2,1)S(1)}, u32[]{:S(2)}, u32[]{:S(2)}) async-start(bf16[2,2,4,8192]{3,2,0,1:T(4,128)(2,1)} %copy.125), calls=%async_computation | async-start | bytes 524288 | tf_op jit(solution)/shard_map/all_to_all | solution.py:83
  13.0 12.2 %all-to-all-start.2 = ((bf16[8,2,2048]{2,1,0:T(2,128)(2,1)}), bf16[8,2,2048]{2,1,0:T(2,128)(2,1)S(1)}, u32[]{:S(2)}, u32[]{:S(2)}) async-start(bf16[8,2,2048]{2,1,0:T(2,128)(2,1)} %bitcast.30), calls=%async_computation.2 | async-start | bytes 131072 | tf_op jit(solution)/shard_map/all_to_all | solution.py:118
  25.2 14.4 %all-to-all-start.1 = ((bf16[8,2,2,4096]{3,2,1,0:T(2,128)(2,1)}), bf16[8,2,2,4096]{3,2,1,0:T(2,128)(2,1)S(1)}, u32[]{:S(2)}, u32[]{:S(2)}) async-start(bf16[8,2,2,4096]{3,2,1,0:T(2,128)(2,1)} %copy.132), calls=%async_computation.1 | async-start | bytes 524288 | tf_op jit(solution)/shard_map/all_to_all | solution.py:115
  31.5 10.1 %collective-permute-start.1 = (bf16[16,2048]{1,0:T(8,128)(2,1)S(1)}, bf16[16,2048]{1,0:T(8,128)(2,1)S(1)}, u32[]{:S(2)}, u32[]{:S(2)}) collective-permute-start(bf16[16,2048]{1,0:T(8,128)(2,1)S(1)} %reshape.312), channel_id=1, source_target_pairs={{0,1},{1,0},{2,3},{3,2},{4,5},{5,4},{6,7},{7,6},{8,9},{9,8},{10,11... | collective-permute-start | bytes 196616 | tf_op jit(solution)/shard_map/ppermute | solution.py:24
  40.2 1.4 collective-permute-start
  47.4 99.0 %all-to-all-start.3 = ((bf16[2,4,256,1024]{2,3,0,1:T(8,128)(2,1)}), bf16[2,4,256,1024]{2,3,0,1:T(8,128)(2,1)}, u32[]{:S(2)}, u32[]{:S(2)}) async-start(bf16[2,4,256,1024]{2,3,0,1:T(8,128)(2,1)} %bitcast.222), calls=%async_computation.3 | async-start | bytes 8388608 | tf_op jit(solution)/shard_map/all_to_all | solution.py:146
  421.7 9.0 %copy-start.1 = (bf16[8,512,128]{2,1,0:T(8,128)(2,1)S(1)}, bf16[8,512,128]{2,1,0:T(8,128)(2,1)}, u32[]{:S(2)}) copy-start(bf16[8,512,128]{2,1,0:T(8,128)(2,1)} %param.5) | copy-start | bytes 3145732
